TPU v7x, 256 devices: a whole 4x4x8 slice. The times are simulated.
256 devices in a mesh: seq: 8 (over z), expert: 8 (over y, core), mp: 4 (over x).
Axes of the slice: x: 4, y: 4, z: 8, core: 2. Of those that a mesh axis runs over, the one named last changes fastest.
Arguments:
- tokens: bfloat16 [2048, 6144], P(('seq', 'expert', 'mp')), may hold values from -6 to 6
- out_grad: bfloat16 [2048, 6144], P(('seq', 'expert', 'mp')), may hold values from -3 to 3
- kept_mask: int32 [2048], P(('seq', 'expert', 'mp')), may hold values 0 or 1
- routes: int32 [2048, 2], P(('seq', 'expert', 'mp')), may hold values from 0 to 7, all different within a row; in each aligned block of 8 rows (0 to 7, 8 to 15, ...) at most 3 rows name the same one
- router: bfloat16 [6144, 8], replicated, may hold values from -0.078125 to 0.078125
- gate_weight: bfloat16 [8, 6144, 8192], P('expert', None, ('seq', 'mp')), may hold values from -0.078125 to 0.078125
- up_weight: bfloat16 [8, 6144, 8192], P('expert', None, ('seq', 'mp')), may hold values from -0.078125 to 0.078125
- down_weight: bfloat16 [8, 8192, 6144], P('expert', ('seq', 'mp')), may hold values from -0.0625 to 0.0625
Outputs:
- d_tokens: bfloat16 [2048, 6144], P(('seq', 'expert', 'mp'))
- gate_grad: float32 [2048, 2], P(('seq', 'expert', 'mp'))
Inputs may be any that keep to these rules, and one draw needn't show every extreme that they name: `routes`: among the 8 rows of one device, at most 3 name any one expert, and in every draw some expert is named by exactly 3 rows of some device.
All inputs are finite; a program needn't handle non-finite values. No bound on the sum of `kept_mask` on one device may be relied on, other than what follows from the above.
Results may differ from a plain program's by a relative error of at most 0.02.
Values may be sent and summed in bfloat16 or wider, within the bound.
A program may use at most 128 MiB of HBM per device.

v0:
```python
import jax
import jax.numpy as jnp
from jax import lax
from jax.sharding import PartitionSpec as P


def on_device(tokens, out_grad, kept_mask, routes, router, gate_weight, up_weight, down_weight):
    row_count = tokens.shape[0]
    width = tokens.shape[1]
    expert_count = lax.axis_size("expert")
    capacity = max(3 * row_count // 8, 2 * row_count // expert_count)
    logits = jnp.dot(tokens, router, preferred_element_type=jnp.float32)
    columns = lax.broadcasted_iota(jnp.int32, (row_count, expert_count), 1)
    first_hot = (routes[:, 0:1] == columns).astype(jnp.float32)
    second_hot = (routes[:, 1:2] == columns).astype(jnp.float32)
    first_logit = jnp.sum(logits * first_hot, axis=1)
    second_logit = jnp.sum(logits * second_hot, axis=1)
    gate_first = jax.nn.sigmoid(first_logit - second_logit)
    gate_second = jax.nn.sigmoid(second_logit - first_logit)
    keep_rows = kept_mask.astype(jnp.float32)
    chosen = ((first_hot + second_hot) * keep_rows[:, None]).astype(jnp.int32)
    position = jnp.cumsum(chosen, axis=0) - 1
    slot_iota = lax.broadcasted_iota(jnp.int32, (row_count, expert_count, capacity), 2)
    select_mask = (chosen[:, :, None] == 1) & (position[:, :, None] == slot_iota)
    select_bf = select_mask.astype(jnp.bfloat16)
    select_full = select_mask.astype(jnp.float32)
    token_send = jnp.einsum(
        "tec,td->ecd", select_bf, tokens, preferred_element_type=jnp.float32
    ).astype(jnp.bfloat16)
    grad_send = jnp.einsum(
        "tec,td->ecd", select_bf, out_grad, preferred_element_type=jnp.float32
    ).astype(jnp.bfloat16)
    gate_table = first_hot * gate_first[:, None] + second_hot * gate_second[:, None]
    gate_send = jnp.einsum(
        "tec,te->ec", select_full, gate_table, precision=lax.Precision.HIGHEST
    ).astype(jnp.bfloat16)
    token_recv, grad_recv, gate_recv = (
        lax.all_to_all(token_send, "expert", split_axis=0, concat_axis=0, tiled=True),
        lax.all_to_all(grad_send, "expert", split_axis=0, concat_axis=0, tiled=True),
        lax.all_to_all(gate_send, "expert", split_axis=0, concat_axis=0, tiled=True),
    )
    token_all, grad_all, gate_all = (
        lax.all_gather(token_recv, ("seq", "mp"), axis=0, tiled=True),
        lax.all_gather(grad_recv, ("seq", "mp"), axis=0, tiled=True),
        lax.all_gather(gate_recv, ("seq", "mp"), axis=0, tiled=True),
    )
    token_all = token_all.reshape(-1, width)
    grad_all = grad_all.reshape(-1, width)
    gate_all = gate_all.reshape(-1)
    gate_local = gate_weight[0]
    up_local = up_weight[0]
    down_local = down_weight[0]
    pre_gate = jnp.dot(token_all, gate_local, preferred_element_type=jnp.float32)
    pre_up = jnp.dot(token_all, up_local, preferred_element_type=jnp.float32)
    sigma = jax.nn.sigmoid(pre_gate)
    act = pre_gate * sigma
    hidden = act * pre_up
    grad_hidden = jnp.dot(grad_all, down_local.T, preferred_element_type=jnp.float32)
    gate_dot = jnp.sum(grad_hidden * hidden, axis=1)
    scaled = gate_all.astype(jnp.float32)[:, None] * grad_hidden
    grad_gate = (scaled * pre_up * sigma * (1.0 + pre_gate * (1.0 - sigma))).astype(jnp.bfloat16)
    grad_up = (scaled * act).astype(jnp.bfloat16)
    expert_grad = jnp.dot(grad_gate, gate_local.T, preferred_element_type=jnp.float32)
    expert_grad = expert_grad + jnp.dot(grad_up, up_local.T, preferred_element_type=jnp.float32)
    grad_own = lax.psum_scatter(
        expert_grad.astype(jnp.bfloat16), ("seq", "mp"), scatter_dimension=0, tiled=True
    ).astype(jnp.float32)
    dot_own = lax.psum_scatter(gate_dot, ("seq", "mp"), scatter_dimension=0, tiled=True)
    grad_back, dot_back = (
        lax.all_to_all(
            grad_own.reshape(expert_count, capacity, width).astype(jnp.bfloat16),
            "expert",
            split_axis=0,
            concat_axis=0,
            tiled=True,
        ).astype(jnp.float32),
        lax.all_to_all(
            dot_own.reshape(expert_count, capacity).astype(jnp.bfloat16),
            "expert",
            split_axis=0,
            concat_axis=0,
            tiled=True,
        ).astype(jnp.float32),
    )
    expert_sum = jnp.einsum("tec,ecd->td", select_full, grad_back, precision=lax.Precision.HIGHEST)
    dot_table = jnp.einsum("tec,ec->te", select_full, dot_back, precision=lax.Precision.HIGHEST)
    dot_first = jnp.sum(dot_table * first_hot, axis=1)
    dot_second = jnp.sum(dot_table * second_hot, axis=1)
    product = gate_first * gate_second * keep_rows
    grad_first = product * (dot_first - dot_second)
    grad_second = product * (dot_second - dot_first)
    logit_grad = first_hot * grad_first[:, None] + second_hot * grad_second[:, None]
    router_term = jnp.dot(logit_grad, router.astype(jnp.float32).T, precision=lax.Precision.HIGHEST)
    d_tokens = ((expert_sum + router_term) * keep_rows[:, None]).astype(jnp.bfloat16)
    gate_grad = jnp.stack([grad_first, grad_second], axis=1)
    return (d_tokens, gate_grad)


def solution(mesh):
    return jax.shard_map(
        on_device,
        mesh=mesh,
        in_specs=(
            P(("seq", "expert", "mp"), None),
            P(("seq", "expert", "mp"), None),
            P(("seq", "expert", "mp")),
            P(("seq", "expert", "mp"), None),
            P(),
            P("expert", None, ("seq", "mp")),
            P("expert", None, ("seq", "mp")),
            P("expert", ("seq", "mp"), None),
        ),
        out_specs=(P(("seq", "expert", "mp"), None), P(("seq", "expert", "mp"), None)),
        check_vma=False,
    )
```

profile of v0, /device:TPU:1, one launch (start us, length us, event | category | flops | bytes accessed | tf_op | source)
XLA Modules:
  0.0 688.7 jit_solution(3209703216275535613)
XLA Ops:
  7.2 0.0 copy-start
  7.2 0.0 all-gather.6.cloned.1.call-start
  7.2 0.8 slice_bitcast_fusion.1
  8.1 0.7 convert_element_type.92
  8.8 0.5 copy-done.5
  9.3 0.2 reduce_window_sum.11
  9.5 0.1 copy.36
  9.6 0.1 copy.35
  9.7 1.2 convolution_convert_fusion
  10.8 0.3 copy.43
  11.1 13.9 %all_to_all.36 = bf16[8,3,6144]{2,1,0:T(4,128)(2,1)S(1)} all-to-all(bf16[8,3,6144]{2,1,0:T(4,128)(2,1)S(1)} %copy.43), channel_id=1, replica_groups=mesh['seq'=8,'expert'=8,'mp'=4] {'expert'}, dimensions={0} | all-to-all | bytes 589824 | tf_op jit(solution)/shard_map/all_to_all | solution.py:38
  24.9 0.9 copy.44
  25.9 0.0 all-gather.6.cloned.1.call-update
  25.9 0.0 all-gather.4.cloned.1.call-start
  26.0 1.2 convolution_convert_fusion.1
  27.1 0.3 copy.39
  27.4 11.3 %all_to_all.37 = bf16[8,3,6144]{2,1,0:T(4,128)(2,1)S(1)} all-to-all(bf16[8,3,6144]{2,1,0:T(4,128)(2,1)S(1)} %copy.39), channel_id=1, replica_groups=mesh['seq'=8,'expert'=8,'mp'=4] {'expert'}, dimensions={0} | all-to-all | bytes 589824 | tf_op jit(solution)/shard_map/all_to_all | solution.py:39
  38.7 0.9 copy.40
  39.7 0.0 all-gather.4.cloned.1.call-update
  39.7 0.0 reduce-scatter.2.cloned.1.call-start
  39.7 1.3 dynamic-slice
  41.7 88.6 %all-gather.6.cloned.1.call-done = bf16[256,3,6144]{2,0,1:T(8,128)(2,1)} async-done(((bf16[8,3,6144]{2,0,1:T(8,128)(2,1)}), bf16[256,3,6144]{2,0,1:T(8,128)(2,1)}) %all-gather.6.cloned.1.call-update) | async-done | bytes 9437200 | tf_op jit(solution)/shard_map/all_gather | solution.py:43
  130.3 14.7 %copy.45 = bf16[256,3,6144]{2,1,0:T(4,128)(2,1)} copy(bf16[256,3,6144]{2,0,1:T(8,128)(2,1)} %all-gather.6.cloned.1.call-done) | data formatting | bytes 18874368 | tf_op jit(solution)/shard_map/all_gather | solution.py:43
  145.0 23.6 %reshape.179 = bf16[768,6144]{1,0:T(8,128)(2,1)} reshape(bf16[256,3,6144]{2,1,0:T(4,128)(2,1)} %copy.45) | data formatting | bytes 18874368 | tf_op jit(solution)/shard_map/reshape | solution.py:47
  168.5 0.0 copy-done
  168.5 7.4 %fusion.4 = f32[768,256]{0,1:T(8,128)} fusion(bf16[768,6144]{1,0:T(8,128)(2,1)} %reshape.179, bf16[1,6144,256]{2,1,0:T(8,128)(2,1)S(1)} %copy-done), kind=kOutput, calls=%fused_computation.9 | convolution fusion | flops 2415919104 | bytes 13369344 | tf_op jit(solution)/shard_map/dot_general | solution.py:53
  175.9 0.0 copy-done.1
  175.9 0.0 copy-done.2
  175.9 3.8 fusion.7
  179.7 53.8 %all-gather.4.cloned.1.call-done = bf16[256,3,6144]{2,0,1:T(8,128)(2,1)} async-done(((bf16[8,3,6144]{2,0,1:T(8,128)(2,1)}), bf16[256,3,6144]{2,0,1:T(8,128)(2,1)}) %all-gather.4.cloned.1.call-update) | async-done | bytes 9437200 | tf_op jit(solution)/shard_map/all_gather | solution.py:44
  233.5 14.7 %copy.41 = bf16[256,3,6144]{2,1,0:T(4,128)(2,1)} copy(bf16[256,3,6144]{2,0,1:T(8,128)(2,1)} %all-gather.4.cloned.1.call-done) | data formatting | bytes 18874368 | tf_op jit(solution)/shard_map/all_gather | solution.py:44
  248.2 23.5 %reshape.178 = bf16[768,6144]{1,0:T(8,128)(2,1)} reshape(bf16[256,3,6144]{2,1,0:T(4,128)(2,1)} %copy.41) | data formatting | bytes 18874368 | tf_op jit(solution)/shard_map/reshape | solution.py:48
  271.7 8.6 %multiply_reduce_fusion = (f32[768]{0:T(1024)S(1)}, f32[768,256]{0,1:T(8,128)}) fusion(f32[768,256]{0,1:T(8,128)} %fusion.7, f32[768,256]{0,1:T(8,128)} %fusion.4, bf16[768,6144]{1,0:T(8,128)(2,1)} %reshape.178, bf16[1,256,6144]{2,1,0:T(8,128)(2,1)} %param.15), kind=kOutput, calls=%fused_computation.16 | convolution fusion | flops 2417294592 | bytes 14945280 | tf_op jit(solution)/shard_map/dot_general | solution.py:58
  280.3 57.6 %all-reduce = bf16[768]{0:T(1024)(128)(2,1)S(1)} all-reduce(f32[768]{0:T(1024)S(1)} %get-tuple-element.13), channel_id=4, replica_groups=mesh['seq'=8,'expert'=8,'mp'=4] {'seq','mp'}, use_global_device_ids=true, to_apply=%region_5.6.clone | all-reduce | flops 768 | bytes 4608
  337.9 0.1 dynamic-slice.3
  337.9 0.1 convert_element_type.108
  338.0 23.4 %all_to_all.38 = bf16[8,1,3]{2,1,0:T(2,128)(2,1)S(1)} all-to-all(bf16[8,1,3]{2,1,0:T(2,128)(2,1)S(1)} %convert_element_type.108), channel_id=1, replica_groups=mesh['seq'=8,'expert'=8,'mp'=4] {'expert'}, dimensions={0} | all-to-all | bytes 96 | tf_op jit(solution)/shard_map/all_to_all | solution.py:77
  361.4 0.1 copy.68
  361.6 0.1 copy.63
  361.6 0.0 copy-done.3
  361.6 0.0 copy-done.4
  361.6 0.2 select_reduce_fusion.3
  361.8 0.0 copy-start.7
  361.8 0.0 copy-start.8
  361.8 0.5 subtract_multiply_fusion.1
  362.4 0.1 copy.64
  362.5 0.1 copy.37
  362.6 7.6 %all_to_all.39 = bf16[8,1,3]{2,1,0:T(2,128)(2,1)S(1)} all-to-all(bf16[8,1,3]{2,1,0:T(2,128)(2,1)S(1)} %copy.37), channel_id=1, replica_groups=mesh['seq'=8,'expert'=8,'mp'=4] {'expert'}, dimensions={0} | all-to-all | bytes 96 | tf_op jit(solution)/shard_map/all_to_all | solution.py:40
  370.2 30.7 %all-gather = bf16[256,1,3]{2,1,0:T(2,128)(2,1)S(1)} all-gather(bf16[8,1,3]{2,1,0:T(2,128)(2,1)S(1)} %all_to_all.39), channel_id=2, replica_groups=mesh['seq'=8,'expert'=8,'mp'=4] {'seq','mp'}, dimensions={0}, use_global_device_ids=true | all-gather | bytes 1584 | tf_op jit(solution)/shard_map/all_gather | solution.py:45
  400.9 0.4 convert_reduce_fusion
  401.3 0.2 reshape.180
  401.5 9.7 %fusion.2 = f32[768,6144]{1,0:T(8,128)} fusion(bf16[1,6144,256]{2,1,0:T(8,128)(2,1)S(1)} %copy-done, f32[768,256]{0,1:T(8,128)} %fusion.4, f32[768,256]{0,1:T(8,128)} %fusion.7, f32[768,256]{0,1:T(8,128)} %get-tuple-element.14, f32[768]{0:T(1024)S(1)} %reshape.180), kind=kOutput, calls=%fused_computation.7 | convolution fusion | flops 2418081792 | bytes 24382464 | tf_op jit(solution)/shard_map/dot_general | solution.py:63
  411.2 0.0 copy-done.8
  411.2 14.2 %add_convert_fusion = bf16[768,6144]{1,0:T(8,128)(2,1)} fusion(f32[768,6144]{1,0:T(8,128)} %fusion.2, bf16[1,6144,256]{2,1,0:T(8,128)(2,1)} %param.14, f32[768,256]{0,1:T(8,128)} %get-tuple-element.14, f32[768]{0:T(1024)S(1)} %reshape.180, f32[768,256]{0,1:T(8,128)} %fusion.4), kind=kOutput, calls=%fused_computation | convolution fusion | flops 2426732544 | bytes 33033216 | tf_op jit(solution)/shard_map/dot_general | solution.py:64
  425.4 0.0 reduce-scatter.2.cloned.1.call-update
  425.5 235.6 %reduce-scatter.2.cloned.1.call-done = bf16[24,6144]{1,0:T(8,128)(2,1)} async-done(((bf16[768,6144]{1,0:T(8,128)(2,1)}), bf16[24,6144]{1,0:T(8,128)(2,1)}) %reduce-scatter.2.cloned.1.call-update) | async-done | bytes 294928 | tf_op jit(solution)/shard_map/reduce_scatter | solution.py:65
  661.1 1.9 convert_element_type.102
  662.9 9.0 %all-to-all-start.3 = ((bf16[8,3,6144]{2,1,0:T(4,128)(2,1)}), bf16[8,3,6144]{2,1,0:T(4,128)(2,1)S(1)}, u32[]{:S(2)}, u32[]{:S(2)}) async-start(bf16[8,3,6144]{2,1,0:T(4,128)(2,1)} %convert_element_type.102), calls=%async_computation.4 | async-start | bytes 786432 | tf_op jit(solution)/shard_map/all_to_all | solution.py:70
  671.9 0.7 subtract_multiply_fusion
  672.6 0.5 copy-done.6
  673.2 1.2 pad_maximum_fusion
  674.3 5.7 all-to-all-done.3
  680.0 0.3 convolution_bitcast_fusion
  680.3 1.8 fusion.1
  (20 shorter events, 0.1 us)
Async XLA Ops:
  7.2 161.4 %copy-start = (bf16[1,6144,256]{2,1,0:T(8,128)(2,1)S(1)}, bf16[1,6144,256]{2,1,0:T(8,128)(2,1)}, u32[]{:S(2)}) copy-start(bf16[1,6144,256]{2,1,0:T(8,128)(2,1)} %param.13) | copy-start | bytes 9437188
  7.2 123.1 %all-gather.6.cloned.1.call-start = ((), (), s32[]{:S(2)}) async-start(), calls=%async_computation.7 | async-start | bytes 9732096 | tf_op jit(solution)/shard_map/all_gather | solution.py:43
  8.8 0.5 copy-start.5
  25.9 207.6 %all-gather.4.cloned.1.call-start = ((), (), s32[]{:S(2)}) async-start(), calls=%async_computation.6 | async-start | bytes 9732096 | tf_op jit(solution)/shard_map/all_gather | solution.py:44
  39.7 621.4 %reduce-scatter.2.cloned.1.call-start = ((), (), s32[]{:S(2)}) async-start(), calls=%async_computation.8 | async-start | bytes 9732096 | tf_op jit(solution)/shard_map/reduce_scatter | solution.py:65
  168.5 7.4 %copy-start.1 = (bf16[768,6144]{1,0:T(8,128)(2,1)S(1)}, bf16[768,6144]{1,0:T(8,128)(2,1)}, u32[]{:S(2)}) copy-start(bf16[768,6144]{1,0:T(8,128)(2,1)} %reshape.179) | copy-start | bytes 28311556
  168.5 7.4 %copy-start.2 = (bf16[1,6144,256]{2,1,0:T(8,128)(2,1)S(1)}, bf16[1,6144,256]{2,1,0:T(8,128)(2,1)}, u32[]{:S(2)}) copy-start(bf16[1,6144,256]{2,1,0:T(8,128)(2,1)} %param.14) | copy-start | bytes 9437188
  271.7 89.9 %copy-start.3 = (bf16[8,6144]{1,0:T(8,128)(2,1)S(1)}, bf16[8,6144]{1,0:T(8,128)(2,1)}, u32[]{:S(2)}) copy-start(bf16[8,6144]{1,0:T(8,128)(2,1)} %param.8) | copy-start | bytes 294916
  271.7 89.9 %copy-start.4 = (bf16[6144,8]{0,1:T(8,128)(2,1)S(1)}, bf16[6144,8]{0,1:T(8,128)(2,1)}, u32[]{:S(2)}) copy-start(bf16[6144,8]{0,1:T(8,128)(2,1)} %param.12) | copy-start | bytes 294916
  271.7 90.1 %copy-start.11 = (s32[8]{0:T(128)S(1)}, s32[8]{0:T(128)}, u32[]{:S(2)}) copy-start(s32[8]{0:T(128)} %param.10) | copy-start | bytes 100
  361.8 49.4 %copy-start.7 = (f32[8]{0:T(128)}, f32[8]{0:T(128)S(1)}, u32[]{:S(2)}) copy-start(f32[8]{0:T(128)S(1)} %get-tuple-element.6) | copy-start | bytes 100
  361.8 49.3 %copy-start.8 = (f32[8]{0:T(128)}, f32[8]{0:T(128)S(1)}, u32[]{:S(2)}) copy-start(f32[8]{0:T(128)S(1)} %get-tuple-element.7) | copy-start | bytes 100
  362.4 48.8 %copy-start.9 = (f32[8]{0:T(128)}, f32[8]{0:T(128)S(1)}, u32[]{:S(2)}) copy-start(f32[8]{0:T(128)S(1)} %get-tuple-element.9) | copy-start | bytes 100
  362.4 48.8 %copy-start.10 = (f32[8]{0:T(128)}, f32[8]{0:T(128)S(1)}, u32[]{:S(2)}) copy-start(f32[8]{0:T(128)S(1)} %get-tuple-element.10) | copy-start | bytes 100
  662.9 17.0 %all-to-all-start.3 = ((bf16[8,3,6144]{2,1,0:T(4,128)(2,1)}), bf16[8,3,6144]{2,1,0:T(4,128)(2,1)S(1)}, u32[]{:S(2)}, u32[]{:S(2)}) async-start(bf16[8,3,6144]{2,1,0:T(4,128)(2,1)} %convert_element_type.102), calls=%async_computation.4 | async-start | bytes 786432 | tf_op jit(solution)/shard_map/all_to_all | solution.py:70
  672.6 0.5 copy-start.6
Sparse Core Ops, SparseCore 0:
  26.0 104.1 all-gather.5
  132.9 100.5 all-gather.3
  425.6 235.4 reduce-scatter.1
where the time goes:
time: 690 us; the launch traced here: 689 us
  waiting for transfers between devices  384 us (56%)
  blocking collectives  144 us (21%)
  local copies, waits for them, and re-layouts  84.8 us (12%)
  matrix products  48.3 us (7%)
  between operations  14.5 us (2%)
  starting transfers between devices  9.09 us (1%)
    reduce_scatter x1, waiting for transfers between devices, on_device(): lax.psum_scatter(expert_grad.astype(jnp.bfloat16), ('seq', 'mp'), scatter...  236 us
    all_gather x1, waiting for transfers between devices, on_device(): lax.all_gather(token_recv, ('seq', 'mp'), axis=0, tiled=True)  88.6 us
    unnamed x1, blocking collectives  57.6 us
    all_gather x1, waiting for transfers between devices, on_device(): lax.all_gather(grad_recv, ('seq', 'mp'), axis=0, tiled=True)  53.8 us
    all_gather x1, blocking collectives, on_device(): lax.all_gather(gate_recv, ('seq', 'mp'), axis=0, tiled=True)  30.7 us
    reshape x1, local copies, waits for them, and re-layouts, on_device(): token_all = token_all.reshape(-1, width)  23.6 us
    reshape x1, local copies, waits for them, and re-layouts, on_device(): grad_all = grad_all.reshape(-1, width)  23.5 us
    all_to_all x1, blocking collectives, on_device(): lax.all_to_all(dot_own.reshape(expert_count, capacity).astype(jnp.bfloat1...  23.4 us
  transfers between devices with their start and end apart: 4, of which 4 were waited for; matrix products, arithmetic and copies ran while one was open for 8% of the time, Pallas kernels for 0%

commit v1 on v0

--- a/solution.py
+++ b/solution.py
@@ -39,10 +39,16 @@
         lax.all_to_all(grad_send, "expert", split_axis=0, concat_axis=0, tiled=True),
         lax.all_to_all(gate_send, "expert", split_axis=0, concat_axis=0, tiled=True),
     )
+    bring_shards_now = lambda z, array_dim: jnp.concatenate(
+        lax.all_to_all(
+            jnp.stack([z for _ in range(lax.psum(1, ("seq", "mp")))], axis=0), ("seq", "mp"), 0, 0
+        ),
+        axis=array_dim,
+    )
     token_all, grad_all, gate_all = (
         lax.all_gather(token_recv, ("seq", "mp"), axis=0, tiled=True),
         lax.all_gather(grad_recv, ("seq", "mp"), axis=0, tiled=True),
-        lax.all_gather(gate_recv, ("seq", "mp"), axis=0, tiled=True),
+        bring_shards_now(gate_recv, 0),
     )
     token_all = token_all.reshape(-1, width)
     grad_all = grad_all.reshape(-1, width)

time: 690 us -> 660 us (0.957)
  blocking collectives: 144 us -> 128 us
  waiting for transfers between devices: 384 us -> 370 us
    all_gather x1 -> x0, blocking collectives: 30.7 us -> none  [on_device(): lax.all_gather(gate_recv, ('seq', 'mp'), axis=0, tiled=True)]
    reduce_scatter x1, waiting for transfers between devices: 236 us -> 221 us  [on_device(): lax.psum_scatter(expert_grad.astype(jnp.bfloat16), ('seq', 'mp'), scatter...]
    all_to_all x0 -> x1, blocking collectives: none -> 14.2 us  [on_device(): lax.all_to_all(jnp.stack([z for _ in range(lax.psum(1, ('seq', 'mp')))],...]
where the time goes in v1:
time: 660 us; the launch traced here: 658 us
  waiting for transfers between devices  370 us (56%)
  blocking collectives  128 us (19%)
  local copies, waits for them, and re-layouts  85.1 us (13%)
  matrix products  48.3 us (7%)
  between operations  14.5 us (2%)
  starting transfers between devices  9.4 us (1%)
    reduce_scatter x1, waiting for transfers between devices, on_device(): lax.psum_scatter(expert_grad.astype(jnp.bfloat16), ('seq', 'mp'), scatter...  221 us
    all_gather x1, waiting for transfers between devices, on_device(): lax.all_gather(token_recv, ('seq', 'mp'), axis=0, tiled=True)  88.6 us
    unnamed x1, blocking collectives  57.6 us
    all_gather x1, waiting for transfers between devices, on_device(): lax.all_gather(grad_recv, ('seq', 'mp'), axis=0, tiled=True)  53.8 us
    reshape x1, local copies, waits for them, and re-layouts, on_device(): token_all = token_all.reshape(-1, width)  23.6 us
    reshape x1, local copies, waits for them, and re-layouts, on_device(): grad_all = grad_all.reshape(-1, width)  23.5 us
    all_to_all x1, blocking collectives, on_device(): lax.all_to_all(dot_own.reshape(expert_count, capacity).astype(jnp.bfloat1...  23.4 us
    all_gather x1, local copies, waits for them, and re-layouts, on_device(): lax.all_gather(token_recv, ('seq', 'mp'), axis=0, tiled=True)  14.7 us
  transfers between devices with their start and end apart: 4, of which 4 were waited for; matrix products, arithmetic and copies ran while one was open for 8% of the time, Pallas kernels for 0%

profile of v1, /device:TPU:1, one launch (start us, length us, event | category | flops | bytes accessed | tf_op | source)
XLA Modules:
  0.0 658.3 jit_solution(3475034274956067598)
XLA Ops:
  7.2 0.0 copy-start
  7.2 0.0 all-gather.5.cloned.1.call-start
  7.2 0.8 slice_bitcast_fusion.1
  8.1 0.7 convert_element_type.92
  8.8 0.5 copy-done.5
  9.3 0.2 reduce_window_sum.11
  9.5 0.1 copy.55
  9.6 0.1 copy.54
  9.7 1.2 convolution_convert_fusion
  10.8 0.3 copy.65
  11.1 13.9 %all_to_all.38 = bf16[8,3,6144]{2,1,0:T(4,128)(2,1)S(1)} all-to-all(bf16[8,3,6144]{2,1,0:T(4,128)(2,1)S(1)} %copy.65), channel_id=1, replica_groups=mesh['seq'=8,'expert'=8,'mp'=4] {'expert'}, dimensions={0} | all-to-all | bytes 589824 | tf_op jit(solution)/shard_map/all_to_all | solution.py:38
  24.9 0.9 copy.66
  25.9 0.0 all-gather.5.cloned.1.call-update
  25.9 0.0 all-gather.3.cloned.1.call-start
  26.0 1.2 convolution_convert_fusion.1
  27.1 0.3 copy.61
  27.4 11.3 %all_to_all.39 = bf16[8,3,6144]{2,1,0:T(4,128)(2,1)S(1)} all-to-all(bf16[8,3,6144]{2,1,0:T(4,128)(2,1)S(1)} %copy.61), channel_id=1, replica_groups=mesh['seq'=8,'expert'=8,'mp'=4] {'expert'}, dimensions={0} | all-to-all | bytes 589824 | tf_op jit(solution)/shard_map/all_to_all | solution.py:39
  38.7 0.9 copy.62
  39.7 0.0 all-gather.3.cloned.1.call-update
  39.7 0.0 reduce-scatter.2.cloned.1.call-start
  39.7 1.3 dynamic-slice
  41.7 88.6 %all-gather.5.cloned.1.call-done = bf16[256,3,6144]{2,0,1:T(8,128)(2,1)} async-done(((bf16[8,3,6144]{2,0,1:T(8,128)(2,1)}), bf16[256,3,6144]{2,0,1:T(8,128)(2,1)}) %all-gather.5.cloned.1.call-update) | async-done | bytes 9437200 | tf_op jit(solution)/shard_map/all_gather | solution.py:49
  130.3 14.7 %copy.67 = bf16[256,3,6144]{2,1,0:T(4,128)(2,1)} copy(bf16[256,3,6144]{2,0,1:T(8,128)(2,1)} %all-gather.5.cloned.1.call-done) | data formatting | bytes 18874368 | tf_op jit(solution)/shard_map/all_gather | solution.py:49
  145.0 23.6 %reshape.181 = bf16[768,6144]{1,0:T(8,128)(2,1)} reshape(bf16[256,3,6144]{2,1,0:T(4,128)(2,1)} %copy.67) | data formatting | bytes 18874368 | tf_op jit(solution)/shard_map/reshape | solution.py:53
  168.5 0.0 copy-done
  168.5 7.4 %fusion.4 = f32[768,256]{0,1:T(8,128)} fusion(bf16[768,6144]{1,0:T(8,128)(2,1)} %reshape.181, bf16[1,6144,256]{2,1,0:T(8,128)(2,1)S(1)} %copy-done), kind=kOutput, calls=%fused_computation.9 | convolution fusion | flops 2415919104 | bytes 13369344 | tf_op jit(solution)/shard_map/dot_general | solution.py:59
  175.9 0.0 copy-done.1
  175.9 0.0 copy-done.2
  175.9 3.8 fusion.7
  179.7 53.8 %all-gather.3.cloned.1.call-done = bf16[256,3,6144]{2,0,1:T(8,128)(2,1)} async-done(((bf16[8,3,6144]{2,0,1:T(8,128)(2,1)}), bf16[256,3,6144]{2,0,1:T(8,128)(2,1)}) %all-gather.3.cloned.1.call-update) | async-done | bytes 9437200 | tf_op jit(solution)/shard_map/all_gather | solution.py:50
  233.5 14.7 %copy.63 = bf16[256,3,6144]{2,1,0:T(4,128)(2,1)} copy(bf16[256,3,6144]{2,0,1:T(8,128)(2,1)} %all-gather.3.cloned.1.call-done) | data formatting | bytes 18874368 | tf_op jit(solution)/shard_map/all_gather | solution.py:50
  248.2 23.5 %reshape.180 = bf16[768,6144]{1,0:T(8,128)(2,1)} reshape(bf16[256,3,6144]{2,1,0:T(4,128)(2,1)} %copy.63) | data formatting | bytes 18874368 | tf_op jit(solution)/shard_map/reshape | solution.py:54
  271.7 8.6 %multiply_reduce_fusion = (f32[768]{0:T(1024)S(1)}, f32[768,256]{0,1:T(8,128)}) fusion(f32[768,256]{0,1:T(8,128)} %fusion.7, f32[768,256]{0,1:T(8,128)} %fusion.4, bf16[768,6144]{1,0:T(8,128)(2,1)} %reshape.180, bf16[1,256,6144]{2,1,0:T(8,128)(2,1)} %param.15), kind=kOutput, calls=%fused_computation.16 | convolution fusion | flops 2417294592 | bytes 14945280 | tf_op jit(solution)/shard_map/dot_general | solution.py:64
  280.3 57.6 %all-reduce = bf16[768]{0:T(1024)(128)(2,1)S(1)} all-reduce(f32[768]{0:T(1024)S(1)} %get-tuple-element.13), channel_id=3, replica_groups=mesh['seq'=8,'expert'=8,'mp'=4] {'seq','mp'}, use_global_device_ids=true, to_apply=%region_5.6.clone | all-reduce | flops 768 | bytes 4608
  337.9 0.1 dynamic-slice.3
  337.9 0.1 convert_element_type.107
  338.0 23.4 %all_to_all.40 = bf16[8,1,3]{2,1,0:T(2,128)(2,1)S(1)} all-to-all(bf16[8,1,3]{2,1,0:T(2,128)(2,1)S(1)} %convert_element_type.107), channel_id=1, replica_groups=mesh['seq'=8,'expert'=8,'mp'=4] {'expert'}, dimensions={0} | all-to-all | bytes 96 | tf_op jit(solution)/shard_map/all_to_all | solution.py:83
  361.4 0.1 copy.90
  361.6 0.1 copy.85
  361.6 0.2 select_reduce_fusion.3
  361.8 0.0 copy-start.7
  361.8 0.0 copy-start.8
  361.8 0.5 subtract_multiply_fusion.1
  362.4 0.1 copy.86
  362.5 0.1 copy.56
  362.6 7.6 %all_to_all.41 = bf16[8,1,3]{2,1,0:T(2,128)(2,1)S(1)} all-to-all(bf16[8,1,3]{2,1,0:T(2,128)(2,1)S(1)} %copy.56), channel_id=1, replica_groups=mesh['seq'=8,'expert'=8,'mp'=4] {'expert'}, dimensions={0} | all-to-all | bytes 96 | tf_op jit(solution)/shard_map/all_to_all | solution.py:40
  370.2 0.1 copy.57
  370.3 14.2 %all_to_all.42 = bf16[32,8,3]{1,2,0:T(4,128)(2,1)S(1)} all-to-all(bf16[32,8,3]{1,2,0:T(4,128)(2,1)S(1)} %stack.7), channel_id=1, replica_groups=mesh['seq'=8,'expert'=8,'mp'=4] {'seq','mp'}, dimensions={0} | all-to-all | bytes 3072 | tf_op jit(solution)/shard_map/all_to_all | solution.py:43
  384.5 0.1 copy.58
  384.6 0.2 copy.59
  384.8 0.2 reshape.182
  385.0 9.7 %fusion.2 = f32[768,6144]{1,0:T(8,128)} fusion(bf16[1,6144,256]{2,1,0:T(8,128)(2,1)S(1)} %copy-done, f32[768,256]{0,1:T(8,128)} %fusion.4, f32[768,256]{0,1:T(8,128)} %fusion.7, f32[768,256]{0,1:T(8,128)} %get-tuple-element.14, f32[768]{0:T(1024)S(1)} %reshape.182), kind=kOutput, calls=%fused_computation.7 | convolution fusion | flops 2418081792 | bytes 24382464 | tf_op jit(solution)/shard_map/dot_general | solution.py:69
  394.7 0.0 copy-done.10
  394.7 14.2 %add_convert_fusion = bf16[768,6144]{1,0:T(8,128)(2,1)} fusion(f32[768,6144]{1,0:T(8,128)} %fusion.2, bf16[1,6144,256]{2,1,0:T(8,128)(2,1)} %param.14, f32[768,256]{0,1:T(8,128)} %get-tuple-element.14, f32[768]{0:T(1024)S(1)} %reshape.182, f32[768,256]{0,1:T(8,128)} %fusion.4), kind=kOutput, calls=%fused_computation | convolution fusion | flops 2426732544 | bytes 33033216 | tf_op jit(solution)/shard_map/dot_general | solution.py:70
  409.0 0.0 reduce-scatter.2.cloned.1.call-update
  409.0 221.4 %reduce-scatter.2.cloned.1.call-done = bf16[24,6144]{1,0:T(8,128)(2,1)} async-done(((bf16[768,6144]{1,0:T(8,128)(2,1)}), bf16[24,6144]{1,0:T(8,128)(2,1)}) %reduce-scatter.2.cloned.1.call-update) | async-done | bytes 294928 | tf_op jit(solution)/shard_map/reduce_scatter | solution.py:71
  630.3 1.9 convert_element_type.102
  632.2 9.3 %all-to-all-start.4 = ((bf16[8,3,6144]{2,1,0:T(4,128)(2,1)}), bf16[8,3,6144]{2,1,0:T(4,128)(2,1)S(1)}, u32[]{:S(2)}, u32[]{:S(2)}) async-start(bf16[8,3,6144]{2,1,0:T(4,128)(2,1)} %convert_element_type.102), calls=%async_computation.5 | async-start | bytes 786432 | tf_op jit(solution)/shard_map/all_to_all | solution.py:76
  641.5 0.7 subtract_multiply_fusion
  642.2 0.5 copy-done.6
  642.7 1.2 pad_maximum_fusion
  643.9 5.7 all-to-all-done.4
  649.6 0.3 convolution_bitcast_fusion
  649.9 1.8 fusion.1
  (23 shorter events, 0.1 us)
Async XLA Ops:
  7.2 161.4 %copy-start = (bf16[1,6144,256]{2,1,0:T(8,128)(2,1)S(1)}, bf16[1,6144,256]{2,1,0:T(8,128)(2,1)}, u32[]{:S(2)}) copy-start(bf16[1,6144,256]{2,1,0:T(8,128)(2,1)} %param.13) | copy-start | bytes 9437188
  7.2 123.1 %all-gather.5.cloned.1.call-start = ((), (), s32[]{:S(2)}) async-start(), calls=%async_computation.8 | async-start | bytes 9732096 | tf_op jit(solution)/shard_map/all_gather | solution.py:49
  8.8 0.5 copy-start.5
  25.9 207.6 %all-gather.3.cloned.1.call-start = ((), (), s32[]{:S(2)}) async-start(), calls=%async_computation.7 | async-start | bytes 9732096 | tf_op jit(solution)/shard_map/all_gather | solution.py:50
  39.7 590.7 %reduce-scatter.2.cloned.1.call-start = ((), (), s32[]{:S(2)}) async-start(), calls=%async_computation.9 | async-start | bytes 9732096 | tf_op jit(solution)/shard_map/reduce_scatter | solution.py:71
  168.5 7.4 %copy-start.1 = (bf16[768,6144]{1,0:T(8,128)(2,1)S(1)}, bf16[768,6144]{1,0:T(8,128)(2,1)}, u32[]{:S(2)}) copy-start(bf16[768,6144]{1,0:T(8,128)(2,1)} %reshape.181) | copy-start | bytes 28311556
  168.5 7.4 %copy-start.2 = (bf16[1,6144,256]{2,1,0:T(8,128)(2,1)S(1)}, bf16[1,6144,256]{2,1,0:T(8,128)(2,1)}, u32[]{:S(2)}) copy-start(bf16[1,6144,256]{2,1,0:T(8,128)(2,1)} %param.14) | copy-start | bytes 9437188
  271.7 89.9 %copy-start.3 = (bf16[8,6144]{1,0:T(8,128)(2,1)S(1)}, bf16[8,6144]{1,0:T(8,128)(2,1)}, u32[]{:S(2)}) copy-start(bf16[8,6144]{1,0:T(8,128)(2,1)} %param.8) | copy-start | bytes 294916
  271.7 89.9 %copy-start.4 = (bf16[6144,8]{0,1:T(8,128)(2,1)S(1)}, bf16[6144,8]{0,1:T(8,128)(2,1)}, u32[]{:S(2)}) copy-start(bf16[6144,8]{0,1:T(8,128)(2,1)} %param.12) | copy-start | bytes 294916
  271.7 90.1 %copy-start.11 = (s32[8]{0:T(128)S(1)}, s32[8]{0:T(128)}, u32[]{:S(2)}) copy-start(s32[8]{0:T(128)} %param.10) | copy-start | bytes 100
  361.8 32.9 %copy-start.7 = (f32[8]{0:T(128)}, f32[8]{0:T(128)S(1)}, u32[]{:S(2)}) copy-start(f32[8]{0:T(128)S(1)} %get-tuple-element.6) | copy-start | bytes 100
  361.8 32.9 %copy-start.8 = (f32[8]{0:T(128)}, f32[8]{0:T(128)S(1)}, u32[]{:S(2)}) copy-start(f32[8]{0:T(128)S(1)} %get-tuple-element.7) | copy-start | bytes 100
  362.4 32.3 %copy-start.9 = (f32[8]{0:T(128)}, f32[8]{0:T(128)S(1)}, u32[]{:S(2)}) copy-start(f32[8]{0:T(128)S(1)} %get-tuple-element.9) | copy-start | bytes 100
  362.4 32.3 %copy-start.10 = (f32[8]{0:T(128)}, f32[8]{0:T(128)S(1)}, u32[]{:S(2)}) copy-start(f32[8]{0:T(128)S(1)} %get-tuple-element.10) | copy-start | bytes 100
  632.2 17.4 %all-to-all-start.4 = ((bf16[8,3,6144]{2,1,0:T(4,128)(2,1)}), bf16[8,3,6144]{2,1,0:T(4,128)(2,1)S(1)}, u32[]{:S(2)}, u32[]{:S(2)}) async-start(bf16[8,3,6144]{2,1,0:T(4,128)(2,1)} %convert_element_type.102), calls=%async_computation.5 | async-start | bytes 786432 | tf_op jit(solution)/shard_map/all_to_all | solution.py:76
  642.2 0.5 copy-start.6
Sparse Core Ops, SparseCore 0:
  26.0 104.1 all-gather.4
  132.9 100.5 all-gather.2
  409.1 221.2 reduce-scatter.1
